TPU v7x, 32 devices: a whole 2x2x4 slice. The times are simulated.
32 devices in a mesh: frame: 4 (over y, x), row: 8 (over z, core).
Axes of the slice: x: 2, y: 2, z: 4, core: 2. Of those that a mesh axis runs over, the one named last changes fastest.
Arguments:
- frames_in: bfloat16 [8, 32, 32, 256], P('frame', 'row'), may hold values from -6 to 6
- conv_first: bfloat16 [3, 3, 256, 256], replicated, may hold values from -0.125 to 0.125
- conv_second: bfloat16 [3, 3, 256, 256], replicated, may hold values from -0.125 to 0.125
- time_kernel: bfloat16 [3, 256, 256], replicated, may hold values from -0.21875 to 0.21875
- norm_gain: float32 [256], replicated, may hold values from 0.1 to 1.9
- w_query: bfloat16 [256, 256], replicated, may hold values from -0.375 to 0.375
- w_key: bfloat16 [256, 256], replicated, may hold values from -0.375 to 0.375
- w_value: bfloat16 [256, 256], replicated, may hold values from -0.375 to 0.375
- w_out: bfloat16 [256, 256], replicated, may hold values from -0.375 to 0.375
- frame_bias: float32 [8, 8], replicated, may hold values from -6 to 400
- conv_third: bfloat16 [3, 3, 256, 256], replicated, may hold values from -0.125 to 0.125
Outputs:
- encoded: bfloat16 [8, 32, 32, 256], P(None, 'row', 'frame')
All inputs are finite; a program needn't handle non-finite values.
Results may differ from a plain program's by a relative error of at most 0.018.
Values may be sent and summed in bfloat16 or wider, within the bound.
A program may use at most 64 MiB of HBM per device.

v0:
```python
import math
import jax
import jax.numpy as jnp
from jax import lax
from jax.sharding import PartitionSpec as P


def extended(cells, sides, width):
    for axis, dim in sides:
        count = lax.axis_size(axis)
        ends = count - 1
        head = lax.slice_in_dim(cells, 0, width, axis=dim)
        tail = lax.slice_in_dim(cells, cells.shape[dim] - width, cells.shape[dim], axis=dim)
        cells = jnp.concatenate(
            [
                lax.ppermute(tail, axis, [(i, (i + 1) % count) for i in range(ends)]),
                cells,
                lax.ppermute(head, axis, [((i + 1) % count, i) for i in range(ends)]),
            ],
            axis=dim,
        )
    return cells


def spatial(padded, weight, row_count, col_count):
    channels = weight.shape[2]
    summed = jnp.zeros((padded.shape[0] * row_count * col_count, weight.shape[3]), jnp.float32)
    for row_tap in range(3):
        for col_tap in range(3):
            window = padded[:, row_tap : row_tap + row_count, col_tap : col_tap + col_count, :]
            summed = summed + jnp.dot(
                window.reshape(-1, channels),
                weight[row_tap, col_tap],
                preferred_element_type=jnp.float32,
            )
    return summed.reshape(padded.shape[0], row_count, col_count, weight.shape[3])


def pad_columns(field):
    return jnp.pad(field, ((0, 0), (0, 0), (1, 1), (0, 0)))


def temporal(moved, time_kernel, norm_gain, w_query, w_key, w_value, w_out, frame_bias):
    frame_count = moved.shape[0]
    channels = moved.shape[-1]
    pixels = moved.reshape(frame_count, -1, channels)
    padded = jnp.pad(pixels, ((1, 1), (0, 0), (0, 0)))
    summed = pixels.astype(jnp.float32)
    for tap in range(3):
        shifted = padded[tap : tap + frame_count].reshape(-1, channels)
        summed = summed + jnp.dot(
            shifted, time_kernel[tap], preferred_element_type=jnp.float32
        ).reshape(pixels.shape)
    timed = summed.astype(jnp.bfloat16)
    widened = timed.astype(jnp.float32)
    scale_inv = lax.rsqrt(jnp.mean(widened * widened, axis=-1, keepdims=True) + 1e-06)
    normed = (widened * scale_inv * norm_gain).astype(jnp.bfloat16).reshape(-1, channels)
    queries = (
        jnp.dot(normed, w_query, preferred_element_type=jnp.float32)
        .astype(jnp.bfloat16)
        .reshape(pixels.shape)
    )
    key_rows = (
        jnp.dot(normed, w_key, preferred_element_type=jnp.float32)
        .astype(jnp.bfloat16)
        .reshape(pixels.shape)
    )
    value_rows = (
        jnp.dot(normed, w_value, preferred_element_type=jnp.float32)
        .astype(jnp.bfloat16)
        .reshape(pixels.shape)
    )
    scores = jnp.einsum(
        "fpc,gpc->pfg", queries, key_rows, preferred_element_type=jnp.float32
    ) / math.sqrt(channels)
    scores = scores + frame_bias
    peak = jnp.max(scores, axis=-1, keepdims=True)
    raised = jnp.exp(scores - peak)
    probs = (raised / jnp.sum(raised, axis=-1, keepdims=True)).astype(jnp.bfloat16)
    context = jnp.einsum(
        "pfg,gpc->fpc", probs, value_rows, preferred_element_type=jnp.float32
    ).astype(jnp.bfloat16)
    projected = jnp.dot(
        context.reshape(-1, channels), w_out, preferred_element_type=jnp.float32
    ).reshape(pixels.shape)
    return (widened + projected).astype(jnp.bfloat16).reshape(moved.shape)


def on_device(
    frames_in,
    conv_first,
    conv_second,
    time_kernel,
    norm_gain,
    w_query,
    w_key,
    w_value,
    w_out,
    frame_bias,
    conv_third,
):
    row_count = frames_in.shape[1]
    col_whole = frames_in.shape[2]
    haloed = extended(frames_in, (("row", 1),), 1)
    first = jax.nn.silu(spatial(pad_columns(haloed), conv_first, row_count, col_whole)).astype(
        jnp.bfloat16
    )
    haloed_two = extended(first, (("row", 1),), 1)
    second = jax.nn.silu(
        spatial(pad_columns(haloed_two), conv_second, row_count, col_whole)
    ).astype(jnp.bfloat16)
    moved = lax.all_to_all(second, "frame", split_axis=2, concat_axis=0, tiled=True)
    attended = temporal(moved, time_kernel, norm_gain, w_query, w_key, w_value, w_out, frame_bias)
    col_count = attended.shape[2]
    framed_last = extended(attended, (("frame", 2), ("row", 1)), 1)
    return spatial(framed_last, conv_third, row_count, col_count).astype(jnp.bfloat16)


def solution(mesh):
    placed = (P("frame", "row", None, None), P(), P(), P(), P(), P(), P(), P(), P(), P(), P())
    return jax.shard_map(
        on_device,
        mesh=mesh,
        in_specs=placed,
        out_specs=P(None, "row", "frame", None),
        check_vma=False,
    )
```

profile of v0, /device:TPU:21, one launch (start us, length us, event | category | flops | bytes accessed | tf_op | source)
XLA Modules:
  0.0 54.3 jit_solution(5470945481003135327)
XLA Ops:
  0.0 0.9 %fusion.102 = (bf16[2,1,32,256]{3,2,1,0:T(8,128)(2,1)S(1)}, bf16[2,1,32,256]{3,2,1,0:T(8,128)(2,1)S(1)}) fusion(bf16[2,4,32,256]{3,2,1,0:T(8,128)(2,1)} %param.11), kind=kLoop, calls=%fused_computation.152 | loop fusion | bytes 131072 | tf_op jit(solution)/shard_map/slice | solution.py:13
  0.9 2.6 %collective-permute-start.1 = (bf16[2,1,32,256]{3,2,1,0:T(8,128)(2,1)S(1)}, bf16[2,1,32,256]{3,2,1,0:T(8,128)(2,1)S(1)}, u32[]{:S(2)}, u32[]{:S(2)}) collective-permute-start(bf16[2,1,32,256]{3,2,1,0:T(8,128)(2,1)S(1)} %get-tuple-element.38), channel_id=1, source_target_pairs={{1,0},{2,1},{3,2},{4,3},{5,4},{6,5},{7,6},{9,8},{10,9},{11,10},{12... | collective-permute-start | bytes 98312 | tf_op jit(solution)/shard_map/ppermute | solution.py:18
  3.5 3.1 %collective-permute-start = (bf16[2,1,32,256]{3,2,1,0:T(8,128)(2,1)S(1)}, bf16[2,1,32,256]{3,2,1,0:T(8,128)(2,1)S(1)}, u32[]{:S(2)}, u32[]{:S(2)}) collective-permute-start(bf16[2,1,32,256]{3,2,1,0:T(8,128)(2,1)S(1)} %get-tuple-element.37), channel_id=1, source_target_pairs={{0,1},{1,2},{2,3},{3,4},{4,5},{5,6},{6,7},{8,9},{9,10},{10,11},{11... | collective-permute-start | bytes 98312 | tf_op jit(solution)/shard_map/ppermute | solution.py:16
  6.6 1.0 %collective-permute-done = bf16[2,1,32,256]{3,2,1,0:T(8,128)(2,1)S(1)} collective-permute-done((bf16[2,1,32,256]{3,2,1,0:T(8,128)(2,1)S(1)}, bf16[2,1,32,256]{3,2,1,0:T(8,128)(2,1)S(1)}, u32[]{:S(2)}, u32[]{:S(2)}) %collective-permute-start) | collective-permute-done | bytes 32800 | tf_op jit(solution)/shard_map/ppermute | solution.py:16
  7.6 1.0 %fusion.19 = bf16[2,6,34,256]{3,2,1,0:T(8,128)(2,1)S(1)} fusion(bf16[2,1,32,256]{3,2,1,0:T(8,128)(2,1)S(1)} %collective-permute-done.1, bf16[2,4,32,256]{3,2,1,0:T(8,128)(2,1)} %param.11, bf16[2,1,32,256]{3,2,1,0:T(8,128)(2,1)S(1)} %collective-permute-done), kind=kLoop, calls=%fused_computation.58 | loop fusion | flops 1253376 | bytes 405504 | tf_op jit(solution)/shard_map/concatenate | solution.py:14
  9.1 0.4 copy-done.1
  11.0 3.2 %collective-permute-start.3 = (bf16[2,1,32,256]{3,2,1,0:T(8,128)(2,1)S(1)}, bf16[2,1,32,256]{3,2,1,0:T(8,128)(2,1)S(1)}, u32[]{:S(2)}, u32[]{:S(2)}) collective-permute-start(bf16[2,1,32,256]{3,2,1,0:T(8,128)(2,1)S(1)} %get-tuple-element.34), channel_id=1, source_target_pairs={{1,0},{2,1},{3,2},{4,3},{5,4},{6,5},{7,6},{9,8},{10,9},{11,10},{12... | collective-permute-start | bytes 98312 | tf_op jit(solution)/shard_map/ppermute | solution.py:18
  14.2 3.1 %collective-permute-start.2 = (bf16[2,1,32,256]{3,2,1,0:T(8,128)(2,1)S(1)}, bf16[2,1,32,256]{3,2,1,0:T(8,128)(2,1)S(1)}, u32[]{:S(2)}, u32[]{:S(2)}) collective-permute-start(bf16[2,1,32,256]{3,2,1,0:T(8,128)(2,1)S(1)} %get-tuple-element.33), channel_id=1, source_target_pairs={{0,1},{1,2},{2,3},{3,4},{4,5},{5,6},{6,7},{8,9},{9,10},{10,11},{11... | collective-permute-start | bytes 98312 | tf_op jit(solution)/shard_map/ppermute | solution.py:16
  17.3 1.0 %collective-permute-done.2 = bf16[2,1,32,256]{3,2,1,0:T(8,128)(2,1)S(1)} collective-permute-done((bf16[2,1,32,256]{3,2,1,0:T(8,128)(2,1)S(1)}, bf16[2,1,32,256]{3,2,1,0:T(8,128)(2,1)S(1)}, u32[]{:S(2)}, u32[]{:S(2)}) %collective-permute-start.2) | collective-permute-done | bytes 32800 | tf_op jit(solution)/shard_map/ppermute | solution.py:16
  19.5 0.2 convolution_add_fusion.12
  20.4 0.8 %copy.24 = bf16[2,4,32,256]{3,1,0,2:T(4,128)(2,1)} copy(bf16[2,4,32,256]{3,2,1,0:T(8,128)(2,1)S(1)} %multiply_convert_fusion.1) | data formatting | bytes 262144 | tf_op jit(solution)/shard_map/convert_element_type | solution.py:111
  21.1 3.7 %all-to-all-start = ((bf16[2,4,32,256]{3,1,0,2:T(4,128)(2,1)}), bf16[2,4,32,256]{3,1,0,2:T(4,128)(2,1)S(1)}, u32[]{:S(2)}, u32[]{:S(2)}) async-start(bf16[2,4,32,256]{3,1,0,2:T(4,128)(2,1)} %copy.24), calls=%async_computation | async-start | bytes 262144 | tf_op jit(solution)/shard_map/all_to_all | solution.py:112
  24.9 3.3 %all-to-all-done = bf16[2,4,32,256]{3,1,0,2:T(4,128)(2,1)S(1)} async-done(((bf16[2,4,32,256]{3,1,0,2:T(4,128)(2,1)}), bf16[2,4,32,256]{3,1,0,2:T(4,128)(2,1)S(1)}, u32[]{:S(2)}, u32[]{:S(2)}) %all-to-all-start) | async-done | bytes 131104 | tf_op jit(solution)/shard_map/all_to_all | solution.py:112
  28.6 0.3 multiply_reduce_fusion
  29.7 0.3 fusion.13
  30.0 0.3 fusion.11
  30.6 2.8 %collective-permute-start.5 = (bf16[8,4,1,256]{3,2,1,0:T(2,128)(2,1)S(1)}, bf16[8,4,1,256]{3,2,1,0:T(2,128)(2,1)S(1)}, u32[]{:S(2)}, u32[]{:S(2)}) collective-permute-start(bf16[8,4,1,256]{3,2,1,0:T(2,128)(2,1)S(1)} %get-tuple-element.30), channel_id=1, source_target_pairs={{8,0},{16,8},{24,16},{9,1},{17,9},{25,17},{10,2},{18,10},{26,18},{... | collective-permute-start | bytes 49160 | tf_op jit(solution)/shard_map/ppermute | solution.py:18
  33.4 2.5 %collective-permute-start.4 = (bf16[8,4,1,256]{3,2,1,0:T(2,128)(2,1)S(1)}, bf16[8,4,1,256]{3,2,1,0:T(2,128)(2,1)S(1)}, u32[]{:S(2)}, u32[]{:S(2)}) collective-permute-start(bf16[8,4,1,256]{3,2,1,0:T(2,128)(2,1)S(1)} %get-tuple-element.29), channel_id=1, source_target_pairs={{0,8},{8,16},{16,24},{1,9},{9,17},{17,25},{2,10},{10,18},{18,26},{... | collective-permute-start | bytes 49160 | tf_op jit(solution)/shard_map/ppermute | solution.py:16
  36.1 2.9 %collective-permute-done.4 = bf16[8,4,1,256]{3,2,1,0:T(2,128)(2,1)S(1)} collective-permute-done((bf16[8,4,1,256]{3,2,1,0:T(2,128)(2,1)S(1)}, bf16[8,4,1,256]{3,2,1,0:T(2,128)(2,1)S(1)}, u32[]{:S(2)}, u32[]{:S(2)}) %collective-permute-start.4) | collective-permute-done | bytes 16416 | tf_op jit(solution)/shard_map/ppermute | solution.py:16
  39.0 7.1 %collective-permute-start.6 = (bf16[8,1,10,256]{3,2,1,0:T(8,128)(2,1)S(1)}, bf16[8,1,10,256]{3,2,1,0:T(8,128)(2,1)S(1)}, u32[]{:S(2)}, u32[]{:S(2)}) collective-permute-start(bf16[8,1,10,256]{3,2,1,0:T(8,128)(2,1)S(1)} %get-tuple-element.25), channel_id=1, source_target_pairs={{0,1},{1,2},{2,3},{3,4},{4,5},{5,6},{6,7},{8,9},{9,10},{10,11},{11... | collective-permute-start | bytes 122888 | tf_op jit(solution)/shard_map/ppermute | solution.py:16
  46.1 1.9 %collective-permute-start.7 = (bf16[8,1,10,256]{3,2,1,0:T(8,128)(2,1)S(1)}, bf16[8,1,10,256]{3,2,1,0:T(8,128)(2,1)S(1)}, u32[]{:S(2)}, u32[]{:S(2)}) collective-permute-start(bf16[8,1,10,256]{3,2,1,0:T(8,128)(2,1)S(1)} %get-tuple-element.26), channel_id=1, source_target_pairs={{1,0},{2,1},{3,2},{4,3},{5,4},{6,5},{7,6},{9,8},{10,9},{11,10},{12... | collective-permute-start | bytes 122888 | tf_op jit(solution)/shard_map/ppermute | solution.py:18
  48.2 3.5 %collective-permute-done.7 = bf16[8,1,10,256]{3,2,1,0:T(8,128)(2,1)S(1)} collective-permute-done((bf16[8,1,10,256]{3,2,1,0:T(8,128)(2,1)S(1)}, bf16[8,1,10,256]{3,2,1,0:T(8,128)(2,1)S(1)}, u32[]{:S(2)}, u32[]{:S(2)}) %collective-permute-start.7) | collective-permute-done | bytes 40992 | tf_op jit(solution)/shard_map/ppermute | solution.py:18
  51.7 0.3 maximum_maximum_fusion
  53.5 0.8 %fusion.7 = bf16[256,256]{1,0:T(8,128)(2,1)} fusion(f32[256,256]{1,0:T(8,128)S(1)} %convolution_add_fusion.3, bf16[256,256]{1,0:T(8,128)(2,1)S(1)} %bitcast.189, bf16[3,3,256,256]{3,2,1,0:T(8,128)(2,1)S(1)} %copy-done.3), kind=kOutput, calls=%fused_computation.30 | convolution fusion | flops 33685504 | bytes 655360 | tf_op jit(solution)/shard_map/dot_general | solution.py:31
  (73 shorter events, 7.1 us)
Async XLA Ops:
  0.0 29.0 %copy-start = (bf16[256,256]{1,0:T(8,128)(2,1)S(1)}, bf16[256,256]{1,0:T(8,128)(2,1)}, u32[]{:S(2)}) copy-start(bf16[256,256]{1,0:T(8,128)(2,1)} %param.18) | copy-start | bytes 393220
  0.0 8.7 %copy-start.2 = (bf16[3,3,256,256]{3,2,1,0:T(8,128)(2,1)S(1)}, bf16[3,3,256,256]{3,2,1,0:T(8,128)(2,1)}, u32[]{:S(2)}) copy-start(bf16[3,3,256,256]{3,2,1,0:T(8,128)(2,1)} %param.12) | copy-start | bytes 3538948
  0.9 5.7 %collective-permute-start.1 = (bf16[2,1,32,256]{3,2,1,0:T(8,128)(2,1)S(1)}, bf16[2,1,32,256]{3,2,1,0:T(8,128)(2,1)S(1)}, u32[]{:S(2)}, u32[]{:S(2)}) collective-permute-start(bf16[2,1,32,256]{3,2,1,0:T(8,128)(2,1)S(1)} %get-tuple-element.38), channel_id=1, source_target_pairs={{1,0},{2,1},{3,2},{4,3},{5,4},{6,5},{7,6},{9,8},{10,9},{11,10},{12... | collective-permute-start | bytes 98312 | tf_op jit(solution)/shard_map/ppermute | solution.py:18
  3.5 4.1 %collective-permute-start = (bf16[2,1,32,256]{3,2,1,0:T(8,128)(2,1)S(1)}, bf16[2,1,32,256]{3,2,1,0:T(8,128)(2,1)S(1)}, u32[]{:S(2)}, u32[]{:S(2)}) collective-permute-start(bf16[2,1,32,256]{3,2,1,0:T(8,128)(2,1)S(1)} %get-tuple-element.37), channel_id=1, source_target_pairs={{0,1},{1,2},{2,3},{3,4},{4,5},{5,6},{6,7},{8,9},{9,10},{10,11},{11... | collective-permute-start | bytes 98312 | tf_op jit(solution)/shard_map/ppermute | solution.py:16
  8.6 0.9 %copy-start.1 = (bf16[2,4,32,256]{3,2,1,0:T(8,128)(2,1)S(1)}, bf16[2,4,32,256]{3,2,1,0:T(8,128)(2,1)}, u32[]{:S(2)}) copy-start(bf16[2,4,32,256]{3,2,1,0:T(8,128)(2,1)} %param.11) | copy-start | bytes 393220
  10.9 7.6 %copy-start.4 = (bf16[3,3,256,256]{3,2,1,0:T(8,128)(2,1)S(1)}, bf16[3,3,256,256]{3,2,1,0:T(8,128)(2,1)}, u32[]{:S(2)}) copy-start(bf16[3,3,256,256]{3,2,1,0:T(8,128)(2,1)} %param.13) | copy-start | bytes 3538948
  11.0 6.3 %collective-permute-start.3 = (bf16[2,1,32,256]{3,2,1,0:T(8,128)(2,1)S(1)}, bf16[2,1,32,256]{3,2,1,0:T(8,128)(2,1)S(1)}, u32[]{:S(2)}, u32[]{:S(2)}) collective-permute-start(bf16[2,1,32,256]{3,2,1,0:T(8,128)(2,1)S(1)} %get-tuple-element.34), channel_id=1, source_target_pairs={{1,0},{2,1},{3,2},{4,3},{5,4},{6,5},{7,6},{9,8},{10,9},{11,10},{12... | collective-permute-start | bytes 98312 | tf_op jit(solution)/shard_map/ppermute | solution.py:18
  14.2 4.1 %collective-permute-start.2 = (bf16[2,1,32,256]{3,2,1,0:T(8,128)(2,1)S(1)}, bf16[2,1,32,256]{3,2,1,0:T(8,128)(2,1)S(1)}, u32[]{:S(2)}, u32[]{:S(2)}) collective-permute-start(bf16[2,1,32,256]{3,2,1,0:T(8,128)(2,1)S(1)} %get-tuple-element.33), channel_id=1, source_target_pairs={{0,1},{1,2},{2,3},{3,4},{4,5},{5,6},{6,7},{8,9},{9,10},{10,11},{11... | collective-permute-start | bytes 98312 | tf_op jit(solution)/shard_map/ppermute | solution.py:16
  20.1 4.7 %copy-start.9 = (f32[8,8]{1,0:T(8,128)S(1)}, f32[8,8]{1,0:T(8,128)}, u32[]{:S(2)}) copy-start(f32[8,8]{1,0:T(8,128)} %param.20) | copy-start | bytes 772
  20.1 8.1 %copy-start.5 = (bf16[3,256,256]{2,1,0:T(8,128)(2,1)S(1)}, bf16[3,256,256]{2,1,0:T(8,128)(2,1)}, u32[]{:S(2)}) copy-start(bf16[3,256,256]{2,1,0:T(8,128)(2,1)} %param.14) | copy-start | bytes 1179652
  21.1 7.0 %all-to-all-start = ((bf16[2,4,32,256]{3,1,0,2:T(4,128)(2,1)}), bf16[2,4,32,256]{3,1,0,2:T(4,128)(2,1)S(1)}, u32[]{:S(2)}, u32[]{:S(2)}) async-start(bf16[2,4,32,256]{3,1,0,2:T(4,128)(2,1)} %copy.24), calls=%async_computation | async-start | bytes 262144 | tf_op jit(solution)/shard_map/all_to_all | solution.py:112
  28.1 0.7 %copy-start.10 = (f32[256]{0:T(256)S(1)}, f32[256]{0:T(256)}, u32[]{:S(2)}) copy-start(f32[256]{0:T(256)} %param.15) | copy-start | bytes 3076
  28.4 0.9 %copy-start.6 = (bf16[256,256]{1,0:T(8,128)(2,1)S(1)}, bf16[256,256]{1,0:T(8,128)(2,1)}, u32[]{:S(2)}) copy-start(bf16[256,256]{1,0:T(8,128)(2,1)} %param.17) | copy-start | bytes 393220
  28.6 0.9 %copy-start.7 = (bf16[256,256]{1,0:T(8,128)(2,1)S(1)}, bf16[256,256]{1,0:T(8,128)(2,1)}, u32[]{:S(2)}) copy-start(bf16[256,256]{1,0:T(8,128)(2,1)} %param.16) | copy-start | bytes 393220
  29.3 1.0 %copy-start.8 = (bf16[256,256]{1,0:T(8,128)(2,1)S(1)}, bf16[256,256]{1,0:T(8,128)(2,1)}, u32[]{:S(2)}) copy-start(bf16[256,256]{1,0:T(8,128)(2,1)} %param.19) | copy-start | bytes 393220
  29.7 6.2 %copy-start.3 = (bf16[3,3,256,256]{3,2,1,0:T(8,128)(2,1)S(1)}, bf16[3,3,256,256]{3,2,1,0:T(8,128)(2,1)}, u32[]{:S(2)}) copy-start(bf16[3,3,256,256]{3,2,1,0:T(8,128)(2,1)} %param.21) | copy-start | bytes 3538948
  30.6 5.5 %collective-permute-start.5 = (bf16[8,4,1,256]{3,2,1,0:T(2,128)(2,1)S(1)}, bf16[8,4,1,256]{3,2,1,0:T(2,128)(2,1)S(1)}, u32[]{:S(2)}, u32[]{:S(2)}) collective-permute-start(bf16[8,4,1,256]{3,2,1,0:T(2,128)(2,1)S(1)} %get-tuple-element.30), channel_id=1, source_target_pairs={{8,0},{16,8},{24,16},{9,1},{17,9},{25,17},{10,2},{18,10},{26,18},{... | collective-permute-start | bytes 49160 | tf_op jit(solution)/shard_map/ppermute | solution.py:18
  33.4 5.6 %collective-permute-start.4 = (bf16[8,4,1,256]{3,2,1,0:T(2,128)(2,1)S(1)}, bf16[8,4,1,256]{3,2,1,0:T(2,128)(2,1)S(1)}, u32[]{:S(2)}, u32[]{:S(2)}) collective-permute-start(bf16[8,4,1,256]{3,2,1,0:T(2,128)(2,1)S(1)} %get-tuple-element.29), channel_id=1, source_target_pairs={{0,8},{8,16},{16,24},{1,9},{9,17},{17,25},{2,10},{10,18},{18,26},{... | collective-permute-start | bytes 49160 | tf_op jit(solution)/shard_map/ppermute | solution.py:16
  39.0 9.2 %collective-permute-start.6 = (bf16[8,1,10,256]{3,2,1,0:T(8,128)(2,1)S(1)}, bf16[8,1,10,256]{3,2,1,0:T(8,128)(2,1)S(1)}, u32[]{:S(2)}, u32[]{:S(2)}) collective-permute-start(bf16[8,1,10,256]{3,2,1,0:T(8,128)(2,1)S(1)} %get-tuple-element.25), channel_id=1, source_target_pairs={{0,1},{1,2},{2,3},{3,4},{4,5},{5,6},{6,7},{8,9},{9,10},{10,11},{11... | collective-permute-start | bytes 122888 | tf_op jit(solution)/shard_map/ppermute | solution.py:16
  46.1 5.6 %collective-permute-start.7 = (bf16[8,1,10,256]{3,2,1,0:T(8,128)(2,1)S(1)}, bf16[8,1,10,256]{3,2,1,0:T(8,128)(2,1)S(1)}, u32[]{:S(2)}, u32[]{:S(2)}) collective-permute-start(bf16[8,1,10,256]{3,2,1,0:T(8,128)(2,1)S(1)} %get-tuple-element.26), channel_id=1, source_target_pairs={{1,0},{2,1},{3,2},{4,3},{5,4},{6,5},{7,6},{9,8},{10,9},{11,10},{12... | collective-permute-start | bytes 122888 | tf_op jit(solution)/shard_map/ppermute | solution.py:18
where the time goes:
time: 54.8 us; the launch traced here: 54.3 us
  starting transfers between devices  29.9 us (55%)
  waiting for transfers between devices  11.6 us (21%)
  matrix products  7.61 us (14%)
  local copies, waits for them, and re-layouts  2.71 us (5%)
  other arithmetic  1.94 us (4%)
  between operations  0.57 us (1%)
    ppermute x4, starting transfers between devices, extended(): lax.ppermute(tail, axis, [(i, (i + 1) % count) for i in range(ends)])  15.8 us
    ppermute x4, starting transfers between devices, extended(): lax.ppermute(head, axis, [((i + 1) % count, i) for i in range(ends)])  10.5 us
    dot_general x27, matrix products, spatial(): jnp.dot(window.reshape(-1, channels), weight[row_tap, col_tap], preferred...  5.71 us
    ppermute x4, waiting for transfers between devices, extended(): lax.ppermute(tail, axis, [(i, (i + 1) % count) for i in range(ends)])  4.84 us
    all_to_all x1, starting transfers between devices, on_device(): lax.all_to_all(second, 'frame', split_axis=2, concat_axis=0, tiled=True)  3.67 us
    ppermute x4, waiting for transfers between devices, extended(): lax.ppermute(head, axis, [((i + 1) % count, i) for i in range(ends)])  3.52 us
    all_to_all x1, waiting for transfers between devices, on_device(): lax.all_to_all(second, 'frame', split_axis=2, concat_axis=0, tiled=True)  3.27 us
    concatenate x6, other arithmetic, extended(): jnp.concatenate([lax.ppermute(tail, axis, [(i, (i + 1) % count) for i in...  1.53 us
  transfers between devices with their start and end apart: 9, of which 5 were waited for; matrix products, arithmetic and copies ran while one was open for 1% of the time, Pallas kernels for 0%

commit v1 on v0

--- a/solution.py
+++ b/solution.py
@@ -3,6 +3,40 @@
 import jax.numpy as jnp
 from jax import lax
 from jax.sharding import PartitionSpec as P
+
+
+def press_the_space(x_local, row_dim, base_x):
+    y1, formed = (x_local.shape[:row_dim], x_local.shape[row_dim + 1 :])
+    out_arr = x_local.reshape(*y1, base_x, -1, *formed)
+    lower = jnp.moveaxis(out_arr, row_dim, 0)
+    return lower
+
+
+def turn_lines(body, dim_k):
+    body = jnp.moveaxis(body, 0, dim_k)
+    block_last = body.shape
+    response = body.reshape(
+        *block_last[:dim_k], block_last[dim_k] * block_last[dim_k + 1], *block_last[dim_k + 2 :]
+    )
+    return response
+
+
+def open_task_on_mesh(unit, axis_key, block_here, piece_in):
+    mixed_arr = lax.axis_index(axis_key)
+    low = lax.axis_size(axis_key)
+    shaped, val = (low, mixed_arr)
+    t_next = press_the_space(unit, block_here, shaped)
+    series = [t_next[val]]
+    for nth in range(1, shaped):
+        z2 = t_next[(val + nth) % shaped]
+        finding = lax.ppermute(
+            z2, axis_name=axis_key, perm=[(t, (t + nth) % shaped) for t in range(shaped)]
+        )
+        series.append(finding)
+    carry = jnp.stack(series)
+    t_next = carry[(val - jnp.arange(shaped)) % shaped]
+    e_now = turn_lines(t_next, piece_in)
+    return e_now
 
 
 def extended(cells, sides, width):
@@ -109,7 +143,7 @@
     second = jax.nn.silu(
         spatial(pad_columns(haloed_two), conv_second, row_count, col_whole)
     ).astype(jnp.bfloat16)
-    moved = lax.all_to_all(second, "frame", split_axis=2, concat_axis=0, tiled=True)
+    moved = open_task_on_mesh(second, "frame", 2, 0)
     attended = temporal(moved, time_kernel, norm_gain, w_query, w_key, w_value, w_out, frame_bias)
     col_count = attended.shape[2]
     framed_last = extended(attended, (("frame", 2), ("row", 1)), 1)

time: 54.8 us -> 52.8 us (0.964)
  starting transfers between devices: 29.9 us -> 28.6 us
    all_to_all x1 -> x0, starting transfers between devices: 3.67 us -> none  [on_device(): lax.all_to_all(second, 'frame', split_axis=2, concat_axis=0, tiled=True)]
    ppermute x0 -> x3, waiting for transfers between devices: none -> 3.65 us  [open_task_on_mesh(): lax.ppermute(z2, axis_name=axis_key, perm=[(t, (t + nth) % shaped) for t...]
    all_to_all x1 -> x0, waiting for transfers between devices: 3.27 us -> none  [on_device(): lax.all_to_all(second, 'frame', split_axis=2, concat_axis=0, tiled=True)]
    ppermute x0 -> x3, starting transfers between devices: none -> 2.45 us  [open_task_on_mesh(): lax.ppermute(z2, axis_name=axis_key, perm=[(t, (t + nth) % shaped) for t...]
    ppermute x4, waiting for transfers between devices: 4.84 us -> 3.92 us  [extended(): lax.ppermute(tail, axis, [(i, (i + 1) % count) for i in range(ends)])]
    ppermute x4, starting transfers between devices: 10.5 us -> 9.59 us  [extended(): lax.ppermute(head, axis, [((i + 1) % count, i) for i in range(ends)])]
    ppermute x4, starting transfers between devices: 15.8 us -> 16.5 us  [extended(): lax.ppermute(tail, axis, [(i, (i + 1) % count) for i in range(ends)])]
    convert_element_type x1 -> x0, local copies, waits for them, and re-layouts: 0.76 us -> none  [on_device(): second = jax.nn.silu(spatial(pad_columns(haloed_two), conv_second, row_co...]
  transfers between devices with their start and end apart: 9 -> 11, of which waited for: 5 -> 7; matrix products, arithmetic and copies ran while one was open for 1% -> 1% of each run, Pallas kernels for 0% -> 0%
where the time goes in v1:
time: 52.8 us; the launch traced here: 52.4 us
  starting transfers between devices  28.6 us (54%)
  waiting for transfers between devices  11.1 us (21%)
  matrix products  7.61 us (14%)
  local copies, waits for them, and re-layouts  2.51 us (5%)
  other arithmetic  1.98 us (4%)
  between operations  0.65 us (1%)
    ppermute x4, starting transfers between devices, extended(): lax.ppermute(tail, axis, [(i, (i + 1) % count) for i in range(ends)])  16.5 us
    ppermute x4, starting transfers between devices, extended(): lax.ppermute(head, axis, [((i + 1) % count, i) for i in range(ends)])  9.59 us
    dot_general x27, matrix products, spatial(): jnp.dot(window.reshape(-1, channels), weight[row_tap, col_tap], preferred...  5.71 us
    ppermute x4, waiting for transfers between devices, extended(): lax.ppermute(tail, axis, [(i, (i + 1) % count) for i in range(ends)])  3.92 us
    ppermute x3, waiting for transfers between devices, open_task_on_mesh(): lax.ppermute(z2, axis_name=axis_key, perm=[(t, (t + nth) % shaped) for t...  3.65 us
    ppermute x4, waiting for transfers between devices, extended(): lax.ppermute(head, axis, [((i + 1) % count, i) for i in range(ends)])  3.52 us
    ppermute x3, starting transfers between devices, open_task_on_mesh(): lax.ppermute(z2, axis_name=axis_key, perm=[(t, (t + nth) % shaped) for t...  2.45 us
    concatenate x6, other arithmetic, extended(): jnp.concatenate([lax.ppermute(tail, axis, [(i, (i + 1) % count) for i in...  1.53 us
  transfers between devices with their start and end apart: 11, of which 7 were waited for; matrix products, arithmetic and copies ran while one was open for 1% of the time, Pallas kernels for 0%

profile of v1, /device:TPU:21, one launch (start us, length us, event | category | flops | bytes accessed | tf_op | source)
XLA Modules:
  0.0 52.4 jit_solution(13487561608668983497)
XLA Ops:
  0.0 0.9 %fusion.105 = (bf16[2,1,32,256]{3,2,1,0:T(8,128)(2,1)S(1)}, bf16[2,1,32,256]{3,2,1,0:T(8,128)(2,1)S(1)}) fusion(bf16[2,4,32,256]{3,2,1,0:T(8,128)(2,1)} %param.11), kind=kLoop, calls=%fused_computation.165 | loop fusion | bytes 131072 | tf_op jit(solution)/shard_map/slice | solution.py:47
  0.9 2.6 %collective-permute-start.1 = (bf16[2,1,32,256]{3,2,1,0:T(8,128)(2,1)S(1)}, bf16[2,1,32,256]{3,2,1,0:T(8,128)(2,1)S(1)}, u32[]{:S(2)}, u32[]{:S(2)}) collective-permute-start(bf16[2,1,32,256]{3,2,1,0:T(8,128)(2,1)S(1)} %get-tuple-element.42), channel_id=1, source_target_pairs={{1,0},{2,1},{3,2},{4,3},{5,4},{6,5},{7,6},{9,8},{10,9},{11,10},{12... | collective-permute-start | bytes 98312 | tf_op jit(solution)/shard_map/ppermute | solution.py:52
  3.5 3.1 %collective-permute-start = (bf16[2,1,32,256]{3,2,1,0:T(8,128)(2,1)S(1)}, bf16[2,1,32,256]{3,2,1,0:T(8,128)(2,1)S(1)}, u32[]{:S(2)}, u32[]{:S(2)}) collective-permute-start(bf16[2,1,32,256]{3,2,1,0:T(8,128)(2,1)S(1)} %get-tuple-element.41), channel_id=1, source_target_pairs={{0,1},{1,2},{2,3},{3,4},{4,5},{5,6},{6,7},{8,9},{9,10},{10,11},{11... | collective-permute-start | bytes 98312 | tf_op jit(solution)/shard_map/ppermute | solution.py:50
  6.6 1.0 %collective-permute-done = bf16[2,1,32,256]{3,2,1,0:T(8,128)(2,1)S(1)} collective-permute-done((bf16[2,1,32,256]{3,2,1,0:T(8,128)(2,1)S(1)}, bf16[2,1,32,256]{3,2,1,0:T(8,128)(2,1)S(1)}, u32[]{:S(2)}, u32[]{:S(2)}) %collective-permute-start) | collective-permute-done | bytes 32800 | tf_op jit(solution)/shard_map/ppermute | solution.py:50
  7.6 1.0 %fusion.18 = bf16[2,6,34,256]{3,2,1,0:T(8,128)(2,1)S(1)} fusion(bf16[2,1,32,256]{3,2,1,0:T(8,128)(2,1)S(1)} %collective-permute-done.1, bf16[2,4,32,256]{3,2,1,0:T(8,128)(2,1)} %param.11, bf16[2,1,32,256]{3,2,1,0:T(8,128)(2,1)S(1)} %collective-permute-done), kind=kLoop, calls=%fused_computation.58 | loop fusion | flops 1253376 | bytes 405504 | tf_op jit(solution)/shard_map/concatenate | solution.py:48
  9.1 0.4 copy-done.1
  11.0 3.2 %collective-permute-start.3 = (bf16[2,1,32,256]{3,2,1,0:T(8,128)(2,1)S(1)}, bf16[2,1,32,256]{3,2,1,0:T(8,128)(2,1)S(1)}, u32[]{:S(2)}, u32[]{:S(2)}) collective-permute-start(bf16[2,1,32,256]{3,2,1,0:T(8,128)(2,1)S(1)} %get-tuple-element.38), channel_id=1, source_target_pairs={{1,0},{2,1},{3,2},{4,3},{5,4},{6,5},{7,6},{9,8},{10,9},{11,10},{12... | collective-permute-start | bytes 98312 | tf_op jit(solution)/shard_map/ppermute | solution.py:52
  14.2 3.1 %collective-permute-start.2 = (bf16[2,1,32,256]{3,2,1,0:T(8,128)(2,1)S(1)}, bf16[2,1,32,256]{3,2,1,0:T(8,128)(2,1)S(1)}, u32[]{:S(2)}, u32[]{:S(2)}) collective-permute-start(bf16[2,1,32,256]{3,2,1,0:T(8,128)(2,1)S(1)} %get-tuple-element.37), channel_id=1, source_target_pairs={{0,1},{1,2},{2,3},{3,4},{4,5},{5,6},{6,7},{8,9},{9,10},{10,11},{11... | collective-permute-start | bytes 98312 | tf_op jit(solution)/shard_map/ppermute | solution.py:50
  17.3 0.9 %collective-permute-done.2 = bf16[2,1,32,256]{3,2,1,0:T(8,128)(2,1)S(1)} collective-permute-done((bf16[2,1,32,256]{3,2,1,0:T(8,128)(2,1)S(1)}, bf16[2,1,32,256]{3,2,1,0:T(8,128)(2,1)S(1)}, u32[]{:S(2)}, u32[]{:S(2)}) %collective-permute-start.2) | collective-permute-done | bytes 32800 | tf_op jit(solution)/shard_map/ppermute | solution.py:50
  20.4 1.2 %collective-permute-start.6 = (bf16[2,4,8,256]{3,2,1,0:T(8,128)(2,1)S(1)}, bf16[2,4,8,256]{3,2,1,0:T(8,128)(2,1)S(1)}, u32[]{:S(2)}, u32[]{:S(2)}) collective-permute-start(bf16[2,4,8,256]{3,2,1,0:T(8,128)(2,1)S(1)} %get-tuple-element.32), channel_id=1, source_target_pairs={{0,24},{8,0},{16,8},{24,16},{1,25},{9,1},{17,9},{25,17},{2,26},{10... | collective-permute-start | bytes 98312 | tf_op jit(solution)/shard_map/ppermute | solution.py:32
  21.6 1.2 %collective-permute-start.5 = (bf16[2,4,8,256]{3,2,1,0:T(8,128)(2,1)S(1)}, bf16[2,4,8,256]{3,2,1,0:T(8,128)(2,1)S(1)}, u32[]{:S(2)}, u32[]{:S(2)}) collective-permute-start(bf16[2,4,8,256]{3,2,1,0:T(8,128)(2,1)S(1)} %get-tuple-element.33), channel_id=1, source_target_pairs={{0,16},{8,24},{16,0},{24,8},{1,17},{9,25},{17,1},{25,9},{2,18},{10... | collective-permute-start | bytes 98312 | tf_op jit(solution)/shard_map/ppermute | solution.py:32
  23.0 0.3 collective-permute-done.6
  23.2 1.2 %collective-permute-done.5 = bf16[2,4,8,256]{3,2,1,0:T(8,128)(2,1)S(1)} collective-permute-done((bf16[2,4,8,256]{3,2,1,0:T(8,128)(2,1)S(1)}, bf16[2,4,8,256]{3,2,1,0:T(8,128)(2,1)S(1)}, u32[]{:S(2)}, u32[]{:S(2)}) %collective-permute-start.5) | collective-permute-done | bytes 32800 | tf_op jit(solution)/shard_map/ppermute | solution.py:32
  24.4 2.2 %collective-permute-done.4 = bf16[2,4,8,256]{3,2,1,0:T(8,128)(2,1)S(1)} collective-permute-done((bf16[2,4,8,256]{3,2,1,0:T(8,128)(2,1)S(1)}, bf16[2,4,8,256]{3,2,1,0:T(8,128)(2,1)S(1)}, u32[]{:S(2)}, u32[]{:S(2)}) %collective-permute-start.4) | collective-permute-done | bytes 32800 | tf_op jit(solution)/shard_map/ppermute | solution.py:32
  26.6 0.6 %gather_fusion = bf16[4,2,4,8,256]{4,3,2,1,0:T(8,128)(2,1)S(1)} fusion(bf16[4,2,4,8,256]{4,3,2,1,0:T(8,128)(2,1)S(1)} %pad_maximum_fusion.7, s32[1024]{0:T(1024)S(1)} %pad_clamp_fusion), kind=kCustom, calls=%fused_computation | custom fusion | bytes 262160 | tf_op jit(solution)/shard_map/gather | solution.py:37
  27.6 0.3 multiply_reduce_fusion
  29.6 1.9 %collective-permute-start.8 = (bf16[8,4,1,256]{3,2,1,0:T(2,128)(2,1)S(1)}, bf16[8,4,1,256]{3,2,1,0:T(2,128)(2,1)S(1)}, u32[]{:S(2)}, u32[]{:S(2)}) collective-permute-start(bf16[8,4,1,256]{3,2,1,0:T(2,128)(2,1)S(1)} %get-tuple-element.30), channel_id=1, source_target_pairs={{8,0},{16,8},{24,16},{9,1},{17,9},{25,17},{10,2},{18,10},{26,18},{... | collective-permute-start | bytes 49160 | tf_op jit(solution)/shard_map/ppermute | solution.py:52
  31.5 3.4 %collective-permute-start.7 = (bf16[8,4,1,256]{3,2,1,0:T(2,128)(2,1)S(1)}, bf16[8,4,1,256]{3,2,1,0:T(2,128)(2,1)S(1)}, u32[]{:S(2)}, u32[]{:S(2)}) collective-permute-start(bf16[8,4,1,256]{3,2,1,0:T(2,128)(2,1)S(1)} %get-tuple-element.29), channel_id=1, source_target_pairs={{0,8},{8,16},{16,24},{1,9},{9,17},{17,25},{2,10},{10,18},{18,26},{... | collective-permute-start | bytes 49160 | tf_op jit(solution)/shard_map/ppermute | solution.py:50
  35.1 2.0 %collective-permute-done.7 = bf16[8,4,1,256]{3,2,1,0:T(2,128)(2,1)S(1)} collective-permute-done((bf16[8,4,1,256]{3,2,1,0:T(2,128)(2,1)S(1)}, bf16[8,4,1,256]{3,2,1,0:T(2,128)(2,1)S(1)}, u32[]{:S(2)}, u32[]{:S(2)}) %collective-permute-start.7) | collective-permute-done | bytes 16416 | tf_op jit(solution)/shard_map/ppermute | solution.py:50
  37.2 7.0 %collective-permute-start.9 = (bf16[8,1,10,256]{3,2,1,0:T(8,128)(2,1)S(1)}, bf16[8,1,10,256]{3,2,1,0:T(8,128)(2,1)S(1)}, u32[]{:S(2)}, u32[]{:S(2)}) collective-permute-start(bf16[8,1,10,256]{3,2,1,0:T(8,128)(2,1)S(1)} %get-tuple-element.25), channel_id=1, source_target_pairs={{0,1},{1,2},{2,3},{3,4},{4,5},{5,6},{6,7},{8,9},{9,10},{10,11},{11... | collective-permute-start | bytes 122888 | tf_op jit(solution)/shard_map/ppermute | solution.py:50
  44.2 1.9 %collective-permute-start.10 = (bf16[8,1,10,256]{3,2,1,0:T(8,128)(2,1)S(1)}, bf16[8,1,10,256]{3,2,1,0:T(8,128)(2,1)S(1)}, u32[]{:S(2)}, u32[]{:S(2)}) collective-permute-start(bf16[8,1,10,256]{3,2,1,0:T(8,128)(2,1)S(1)} %get-tuple-element.26), channel_id=1, source_target_pairs={{1,0},{2,1},{3,2},{4,3},{5,4},{6,5},{7,6},{9,8},{10,9},{11,10},{12... | collective-permute-start | bytes 122888 | tf_op jit(solution)/shard_map/ppermute | solution.py:52
  46.2 3.5 %collective-permute-done.10 = bf16[8,1,10,256]{3,2,1,0:T(8,128)(2,1)S(1)} collective-permute-done((bf16[8,1,10,256]{3,2,1,0:T(8,128)(2,1)S(1)}, bf16[8,1,10,256]{3,2,1,0:T(8,128)(2,1)S(1)}, u32[]{:S(2)}, u32[]{:S(2)}) %collective-permute-start.10) | collective-permute-done | bytes 40992 | tf_op jit(solution)/shard_map/ppermute | solution.py:52
  49.8 0.3 maximum_maximum_fusion
  51.6 0.8 %fusion.7 = bf16[256,256]{1,0:T(8,128)(2,1)} fusion(f32[256,256]{1,0:T(8,128)S(1)} %convolution_add_fusion.3, bf16[256,256]{1,0:T(8,128)(2,1)S(1)} %bitcast.200, bf16[3,3,256,256]{3,2,1,0:T(8,128)(2,1)S(1)} %copy-done.3), kind=kOutput, calls=%fused_computation.31 | convolution fusion | flops 33685504 | bytes 655360 | tf_op jit(solution)/shard_map/dot_general | solution.py:65
  (80 shorter events, 7.9 us)
Async XLA Ops:
  0.0 28.0 %copy-start = (bf16[256,256]{1,0:T(8,128)(2,1)S(1)}, bf16[256,256]{1,0:T(8,128)(2,1)}, u32[]{:S(2)}) copy-start(bf16[256,256]{1,0:T(8,128)(2,1)} %param.18) | copy-start | bytes 393220
  0.0 8.7 %copy-start.2 = (bf16[3,3,256,256]{3,2,1,0:T(8,128)(2,1)S(1)}, bf16[3,3,256,256]{3,2,1,0:T(8,128)(2,1)}, u32[]{:S(2)}) copy-start(bf16[3,3,256,256]{3,2,1,0:T(8,128)(2,1)} %param.12) | copy-start | bytes 3538948
  0.9 5.7 %collective-permute-start.1 = (bf16[2,1,32,256]{3,2,1,0:T(8,128)(2,1)S(1)}, bf16[2,1,32,256]{3,2,1,0:T(8,128)(2,1)S(1)}, u32[]{:S(2)}, u32[]{:S(2)}) collective-permute-start(bf16[2,1,32,256]{3,2,1,0:T(8,128)(2,1)S(1)} %get-tuple-element.42), channel_id=1, source_target_pairs={{1,0},{2,1},{3,2},{4,3},{5,4},{6,5},{7,6},{9,8},{10,9},{11,10},{12... | collective-permute-start | bytes 98312 | tf_op jit(solution)/shard_map/ppermute | solution.py:52
  3.5 4.1 %collective-permute-start = (bf16[2,1,32,256]{3,2,1,0:T(8,128)(2,1)S(1)}, bf16[2,1,32,256]{3,2,1,0:T(8,128)(2,1)S(1)}, u32[]{:S(2)}, u32[]{:S(2)}) collective-permute-start(bf16[2,1,32,256]{3,2,1,0:T(8,128)(2,1)S(1)} %get-tuple-element.41), channel_id=1, source_target_pairs={{0,1},{1,2},{2,3},{3,4},{4,5},{5,6},{6,7},{8,9},{9,10},{10,11},{11... | collective-permute-start | bytes 98312 | tf_op jit(solution)/shard_map/ppermute | solution.py:50
  8.6 0.9 %copy-start.1 = (bf16[2,4,32,256]{3,2,1,0:T(8,128)(2,1)S(1)}, bf16[2,4,32,256]{3,2,1,0:T(8,128)(2,1)}, u32[]{:S(2)}) copy-start(bf16[2,4,32,256]{3,2,1,0:T(8,128)(2,1)} %param.11) | copy-start | bytes 393220
  10.9 7.5 %copy-start.4 = (bf16[3,3,256,256]{3,2,1,0:T(8,128)(2,1)S(1)}, bf16[3,3,256,256]{3,2,1,0:T(8,128)(2,1)}, u32[]{:S(2)}) copy-start(bf16[3,3,256,256]{3,2,1,0:T(8,128)(2,1)} %param.13) | copy-start | bytes 3538948
  11.0 6.4 %collective-permute-start.3 = (bf16[2,1,32,256]{3,2,1,0:T(8,128)(2,1)S(1)}, bf16[2,1,32,256]{3,2,1,0:T(8,128)(2,1)S(1)}, u32[]{:S(2)}, u32[]{:S(2)}) collective-permute-start(bf16[2,1,32,256]{3,2,1,0:T(8,128)(2,1)S(1)} %get-tuple-element.38), channel_id=1, source_target_pairs={{1,0},{2,1},{3,2},{4,3},{5,4},{6,5},{7,6},{9,8},{10,9},{11,10},{12... | collective-permute-start | bytes 98312 | tf_op jit(solution)/shard_map/ppermute | solution.py:52
  14.2 4.1 %collective-permute-start.2 = (bf16[2,1,32,256]{3,2,1,0:T(8,128)(2,1)S(1)}, bf16[2,1,32,256]{3,2,1,0:T(8,128)(2,1)S(1)}, u32[]{:S(2)}, u32[]{:S(2)}) collective-permute-start(bf16[2,1,32,256]{3,2,1,0:T(8,128)(2,1)S(1)} %get-tuple-element.37), channel_id=1, source_target_pairs={{0,1},{1,2},{2,3},{3,4},{4,5},{5,6},{6,7},{8,9},{9,10},{10,11},{11... | collective-permute-start | bytes 98312 | tf_op jit(solution)/shard_map/ppermute | solution.py:50
  19.9 3.0 %copy-start.9 = (f32[8,8]{1,0:T(8,128)S(1)}, f32[8,8]{1,0:T(8,128)}, u32[]{:S(2)}) copy-start(f32[8,8]{1,0:T(8,128)} %param.20) | copy-start | bytes 772
  20.1 7.1 %copy-start.5 = (bf16[3,256,256]{2,1,0:T(8,128)(2,1)S(1)}, bf16[3,256,256]{2,1,0:T(8,128)(2,1)}, u32[]{:S(2)}) copy-start(bf16[3,256,256]{2,1,0:T(8,128)(2,1)} %param.14) | copy-start | bytes 1179652
  20.4 2.8 %collective-permute-start.6 = (bf16[2,4,8,256]{3,2,1,0:T(8,128)(2,1)S(1)}, bf16[2,4,8,256]{3,2,1,0:T(8,128)(2,1)S(1)}, u32[]{:S(2)}, u32[]{:S(2)}) collective-permute-start(bf16[2,4,8,256]{3,2,1,0:T(8,128)(2,1)S(1)} %get-tuple-element.32), channel_id=1, source_target_pairs={{0,24},{8,0},{16,8},{24,16},{1,25},{9,1},{17,9},{25,17},{2,26},{10... | collective-permute-start | bytes 98312 | tf_op jit(solution)/shard_map/ppermute | solution.py:32
  21.6 2.8 %collective-permute-start.5 = (bf16[2,4,8,256]{3,2,1,0:T(8,128)(2,1)S(1)}, bf16[2,4,8,256]{3,2,1,0:T(8,128)(2,1)S(1)}, u32[]{:S(2)}, u32[]{:S(2)}) collective-permute-start(bf16[2,4,8,256]{3,2,1,0:T(8,128)(2,1)S(1)} %get-tuple-element.33), channel_id=1, source_target_pairs={{0,16},{8,24},{16,0},{24,8},{1,17},{9,25},{17,1},{25,9},{2,18},{10... | collective-permute-start | bytes 98312 | tf_op jit(solution)/shard_map/ppermute | solution.py:32
  22.9 3.7 %collective-permute-start.4 = (bf16[2,4,8,256]{3,2,1,0:T(8,128)(2,1)S(1)}, bf16[2,4,8,256]{3,2,1,0:T(8,128)(2,1)S(1)}, u32[]{:S(2)}, u32[]{:S(2)}) collective-permute-start(bf16[2,4,8,256]{3,2,1,0:T(8,128)(2,1)S(1)} %get-tuple-element.34), channel_id=1, source_target_pairs={{0,8},{8,16},{16,24},{24,0},{1,9},{9,17},{17,25},{25,1},{2,10},{10... | collective-permute-start | bytes 98312 | tf_op jit(solution)/shard_map/ppermute | solution.py:32
  26.6 1.3 %copy-start.10 = (f32[256]{0:T(256)S(1)}, f32[256]{0:T(256)}, u32[]{:S(2)}) copy-start(f32[256]{0:T(256)} %param.15) | copy-start | bytes 3076
  27.4 0.9 %copy-start.6 = (bf16[256,256]{1,0:T(8,128)(2,1)S(1)}, bf16[256,256]{1,0:T(8,128)(2,1)}, u32[]{:S(2)}) copy-start(bf16[256,256]{1,0:T(8,128)(2,1)} %param.17) | copy-start | bytes 393220
  27.6 0.9 %copy-start.7 = (bf16[256,256]{1,0:T(8,128)(2,1)S(1)}, bf16[256,256]{1,0:T(8,128)(2,1)}, u32[]{:S(2)}) copy-start(bf16[256,256]{1,0:T(8,128)(2,1)} %param.16) | copy-start | bytes 393220
  28.3 1.0 %copy-start.8 = (bf16[256,256]{1,0:T(8,128)(2,1)S(1)}, bf16[256,256]{1,0:T(8,128)(2,1)}, u32[]{:S(2)}) copy-start(bf16[256,256]{1,0:T(8,128)(2,1)} %param.19) | copy-start | bytes 393220
  28.7 6.2 %copy-start.3 = (bf16[3,3,256,256]{3,2,1,0:T(8,128)(2,1)S(1)}, bf16[3,3,256,256]{3,2,1,0:T(8,128)(2,1)}, u32[]{:S(2)}) copy-start(bf16[3,3,256,256]{3,2,1,0:T(8,128)(2,1)} %param.21) | copy-start | bytes 3538948
  29.6 5.5 %collective-permute-start.8 = (bf16[8,4,1,256]{3,2,1,0:T(2,128)(2,1)S(1)}, bf16[8,4,1,256]{3,2,1,0:T(2,128)(2,1)S(1)}, u32[]{:S(2)}, u32[]{:S(2)}) collective-permute-start(bf16[8,4,1,256]{3,2,1,0:T(2,128)(2,1)S(1)} %get-tuple-element.30), channel_id=1, source_target_pairs={{8,0},{16,8},{24,16},{9,1},{17,9},{25,17},{10,2},{18,10},{26,18},{... | collective-permute-start | bytes 49160 | tf_op jit(solution)/shard_map/ppermute | solution.py:52
  31.5 5.6 %collective-permute-start.7 = (bf16[8,4,1,256]{3,2,1,0:T(2,128)(2,1)S(1)}, bf16[8,4,1,256]{3,2,1,0:T(2,128)(2,1)S(1)}, u32[]{:S(2)}, u32[]{:S(2)}) collective-permute-start(bf16[8,4,1,256]{3,2,1,0:T(2,128)(2,1)S(1)} %get-tuple-element.29), channel_id=1, source_target_pairs={{0,8},{8,16},{16,24},{1,9},{9,17},{17,25},{2,10},{10,18},{18,26},{... | collective-permute-start | bytes 49160 | tf_op jit(solution)/shard_map/ppermute | solution.py:50
  37.2 9.0 %collective-permute-start.9 = (bf16[8,1,10,256]{3,2,1,0:T(8,128)(2,1)S(1)}, bf16[8,1,10,256]{3,2,1,0:T(8,128)(2,1)S(1)}, u32[]{:S(2)}, u32[]{:S(2)}) collective-permute-start(bf16[8,1,10,256]{3,2,1,0:T(8,128)(2,1)S(1)} %get-tuple-element.25), channel_id=1, source_target_pairs={{0,1},{1,2},{2,3},{3,4},{4,5},{5,6},{6,7},{8,9},{9,10},{10,11},{11... | collective-permute-start | bytes 122888 | tf_op jit(solution)/shard_map/ppermute | solution.py:50
  44.2 5.6 %collective-permute-start.10 = (bf16[8,1,10,256]{3,2,1,0:T(8,128)(2,1)S(1)}, bf16[8,1,10,256]{3,2,1,0:T(8,128)(2,1)S(1)}, u32[]{:S(2)}, u32[]{:S(2)}) collective-permute-start(bf16[8,1,10,256]{3,2,1,0:T(8,128)(2,1)S(1)} %get-tuple-element.26), channel_id=1, source_target_pairs={{1,0},{2,1},{3,2},{4,3},{5,4},{6,5},{7,6},{9,8},{10,9},{11,10},{12... | collective-permute-start | bytes 122888 | tf_op jit(solution)/shard_map/ppermute | solution.py:52
